TPU v7x, 256 devices: a whole 4x4x8 slice. The times are simulated.
256 devices in a mesh: seq: 32 (over z, y), head: 2 (over core), dp: 4 (over x).
Axes of the slice: x: 4, y: 4, z: 8, core: 2. Of those that a mesh axis runs over, the one named last changes fastest.
Arguments:
- queries: bfloat16 [90112, 2048], P(('dp', 'seq'), 'head'), parts along dimension 0, may hold values from -96 to 96
- out_grad: bfloat16 [90112, 2048], P(('dp', 'seq'), 'head'), parts along dimension 0, may hold values from -16 to 16
- encodings: bfloat16 [1280, 16, 2048], P(('dp', 'seq'), None, 'head'), parts along dimension 0, may hold values from -6 to 6
- key_weight: bfloat16 [2048, 2048], P(None, 'head'), may hold values from -0.125 to 0.125
- value_weight: bfloat16 [2048, 2048], P(None, 'head'), may hold values from -0.125 to 0.125
- neighbours: int32 [1408, 2], P(('dp', 'seq')), parts along dimension 0, may hold values from 0 to 319, as said below
Outputs:
- query_grad: bfloat16 [90112, 2048], P(('dp', 'seq'), 'head'), parts along dimension 0
- encoding_grad: bfloat16 [1280, 16, 2048], P(('dp', 'seq'), None, 'head'), parts along dimension 0
There are 4 independent parts, one for each index of `dp`. A program takes and returns all parts, laid end to end along the dimension named above; an argument that names none is the same for every part. Nothing has to cross between parts.
Inputs may be any that keep to these rules, and one draw needn't show every extreme that they name: `neighbours`: row r of encodings is held by index r // 10 of seq. In each aligned block of 11 spans, at most 2 of the 22 ids belong to one holder, and some holder has exactly 2. A span's two ids differ.
All inputs are finite; a program needn't handle non-finite values.
Results may differ from a plain program's by a relative error of at most 0.011.
Values may be sent and summed in bfloat16 or wider, within the bound.
No kernel may reach another device: no remote copies, remote signals or barrier semaphores. Data moves between devices by JAX's collectives and lax.ppermute only.
A program may use at most 64 MiB of HBM per device.

v0:
```python
import math
import jax
import jax.numpy as jnp
from jax import lax
from jax.sharding import PartitionSpec as P

D = 2048
HEADS = 16


def slot_ranks(owner_ids):
    count = owner_ids.shape[-1]
    same_owner = owner_ids[..., :, None] == owner_ids[..., None, :]
    positions = jnp.arange(count, dtype=jnp.int32)
    earlier = positions[None, :] < positions[:, None]
    return jnp.sum(same_owner & earlier, axis=-1)


def on_device(queries, out_grad, encodings, key_weight, value_weight, neighbours):
    seq_count = lax.axis_size("seq")
    seq_index = lax.axis_index("seq")
    spans_here = neighbours.shape[0]
    ref_count = 2 * spans_here
    rows_here, neighbour_len, half_width = encodings.shape
    full_width = key_weight.shape[0]
    tok_rows = queries.shape[0]
    span_len = tok_rows // spans_here
    head_size = D // HEADS
    heads_here = half_width // head_size
    scaling = 1.0 / math.sqrt(head_size)
    capacity = max(2, ref_count // seq_count)
    slot_count = seq_count * capacity
    all_lists = lax.all_gather(neighbours, "seq", axis=0, tiled=True).reshape(seq_count, ref_count)
    owner_table = all_lists // rows_here
    local_table = all_lists % rows_here
    rank_table = slot_ranks(owner_table)
    own_ids = neighbours.reshape(ref_count)
    own_owner = own_ids // rows_here
    position = own_owner * capacity + slot_ranks(own_owner)
    slot_ids = jnp.arange(capacity, dtype=jnp.int32)
    chosen = (owner_table == seq_index)[:, None, :] & (
        rank_table[:, None, :] == slot_ids[None, :, None]
    )
    filled = jnp.any(chosen, axis=-1)
    slot_row = jnp.sum(jnp.where(chosen, local_table[:, None, :], 0), axis=-1)
    select = filled[..., None] & (
        slot_row[..., None] == jnp.arange(rows_here, dtype=jnp.int32)[None, None, :]
    )
    select = select.astype(jnp.bfloat16).reshape(slot_count, rows_here)
    flat_enc = encodings.reshape(rows_here, neighbour_len * half_width)
    outgoing = jnp.dot(select, flat_enc, preferred_element_type=jnp.float32).astype(jnp.bfloat16)
    outgoing = outgoing.reshape(seq_count, capacity, neighbour_len, half_width)
    arrived = lax.all_to_all(outgoing, "seq", split_axis=0, concat_axis=0, tiled=True)
    flat_arrived = arrived.reshape(slot_count, neighbour_len, half_width)
    whole = lax.all_gather(flat_arrived, "head", axis=2, tiled=True)
    full_rows = jnp.take(whole, position, axis=0)
    flat_rows = full_rows.reshape(ref_count * neighbour_len, full_width)
    keys = jnp.dot(flat_rows, key_weight, preferred_element_type=jnp.float32).astype(jnp.bfloat16)
    values = jnp.dot(flat_rows, value_weight, preferred_element_type=jnp.float32).astype(
        jnp.bfloat16
    )
    query_heads = queries.reshape(spans_here, span_len, heads_here, head_size)
    grad_heads = out_grad.reshape(spans_here, span_len, heads_here, head_size)
    key_heads = keys.reshape(spans_here, 2 * neighbour_len, heads_here, head_size)
    value_heads = values.reshape(spans_here, 2 * neighbour_len, heads_here, head_size)
    scores = (
        jnp.einsum("cthd,cuhd->chtu", query_heads, key_heads, preferred_element_type=jnp.float32)
        * scaling
    )
    scores = scores - jnp.max(scores, axis=-1, keepdims=True)
    raised = jnp.exp(scores)
    probs = raised / jnp.sum(raised, axis=-1, keepdims=True)
    probs_b = probs.astype(jnp.bfloat16)
    attended = jnp.einsum(
        "chtu,cuhd->cthd", probs_b, value_heads, preferred_element_type=jnp.float32
    )
    delta = jnp.transpose(jnp.sum(grad_heads.astype(jnp.float32) * attended, axis=-1), (0, 2, 1))
    dprobs = jnp.einsum(
        "cthd,cuhd->chtu", grad_heads, value_heads, preferred_element_type=jnp.float32
    )
    dscores = (probs * (dprobs - delta[..., None])).astype(jnp.bfloat16)
    query_grad = (
        jnp.einsum("chtu,cuhd->cthd", dscores, key_heads, preferred_element_type=jnp.float32)
        * scaling
    )
    query_grad = query_grad.astype(jnp.bfloat16).reshape(tok_rows, half_width)
    key_grad = (
        jnp.einsum("chtu,cthd->cuhd", dscores, query_heads, preferred_element_type=jnp.float32)
        * scaling
    )
    key_grad = key_grad.astype(jnp.bfloat16).reshape(ref_count * neighbour_len, half_width)
    value_grad = jnp.einsum(
        "chtu,cthd->cuhd", probs_b, grad_heads, preferred_element_type=jnp.float32
    )
    value_grad = value_grad.astype(jnp.bfloat16).reshape(ref_count * neighbour_len, half_width)
    contract = (((1,), (1,)), ((), ()))
    partial_value = lax.dot_general(
        key_grad, key_weight, contract, preferred_element_type=jnp.float32
    )
    partial_value = partial_value + lax.dot_general(
        value_grad, value_weight, contract, preferred_element_type=jnp.float32
    )
    summed = lax.psum_scatter(
        partial_value.reshape(ref_count, neighbour_len, full_width),
        "head",
        scatter_dimension=2,
        tiled=True,
    )
    ref_grad = summed.astype(jnp.bfloat16)
    returning = (
        jnp.zeros((slot_count, neighbour_len, half_width), jnp.bfloat16).at[position].set(ref_grad)
    )
    returning = returning.reshape(seq_count, capacity, neighbour_len, half_width)
    came_back = lax.all_to_all(returning, "seq", split_axis=0, concat_axis=0, tiled=True).reshape(
        slot_count, neighbour_len * half_width
    )
    encoding_grad = lax.dot_general(
        select, came_back, (((0,), (0,)), ((), ())), preferred_element_type=jnp.float32
    )
    encoding_grad = encoding_grad.astype(jnp.bfloat16).reshape(rows_here, neighbour_len, half_width)
    return (query_grad, encoding_grad)


def solution(mesh):
    return jax.shard_map(
        on_device,
        mesh=mesh,
        in_specs=(
            P(("dp", "seq"), "head"),
            P(("dp", "seq"), "head"),
            P(("dp", "seq"), None, "head"),
            P(None, "head"),
            P(None, "head"),
            P(("dp", "seq"), None),
        ),
        out_specs=(P(("dp", "seq"), "head"), P(("dp", "seq"), None, "head")),
        check_vma=False,
    )
```

profile of v0, /device:TPU:2, one launch (start us, length us, event | category | flops | bytes accessed | tf_op | source)
XLA Modules:
  0.0 242.0 jit_solution(4702923652695932510)
XLA Ops:
  7.2 0.0 all-gather.3.cloned.1.call-start
  7.2 46.3 %all-gather = s32[32,11,2]{1,2,0:T(2,128)S(1)} all-gather(s32[1,11,2]{1,2,0:T(2,128)} %bitcast.115), channel_id=1, replica_groups=mesh['seq'=32,'head'=2,'dp'=4] {'seq'}, dimensions={0}, use_global_device_ids=true | all-gather | bytes 2904 | tf_op jit(solution)/shard_map/all_gather | solution.py:33
  53.5 0.1 copy.88
  53.8 0.2 convert_reduce_fusion
  54.0 0.1 copy.93
  54.1 0.1 eq.78
  54.2 0.1 copy.92
  54.3 0.1 and.96
  54.4 1.0 pad.1
  55.5 0.3 copy.109
  55.8 0.7 convolution_convert_fusion
  56.5 1.2 copy.110
  57.7 46.8 %all_to_all.10 = bf16[32,2,16,1024]{3,2,1,0:T(8,128)(2,1)} all-to-all(bf16[32,2,16,1024]{3,2,1,0:T(8,128)(2,1)S(1)} %bitcast.94), channel_id=1, replica_groups=mesh['seq'=32,'head'=2,'dp'=4] {'seq'}, dimensions={0} | all-to-all | bytes 4194304 | tf_op jit(solution)/shard_map/all_to_all | solution.py:53
  104.5 0.0 all-gather.3.cloned.1.call-update
  104.6 0.2 reduce-scatter.2.cloned.1.call-start
  104.8 0.4 copy-done.5
  105.2 0.1 copy.87
  105.3 0.1 div.57
  105.4 0.1 div.60
  105.5 0.1 copy.86
  105.6 0.1 and.88
  105.7 0.1 and.100
  105.8 0.2 convert_reduce_fusion.1
  106.0 0.1 broadcast_in_dim.25
  106.1 0.1 broadcast_in_dim.26
  106.2 0.0 copy-start.1
  106.2 0.4 copy.112
  106.6 0.9 copy-done.1
  107.6 1.5 copy.114
  109.1 11.6 %all-gather.3.cloned.1.call-done = bf16[64,16,2048]{2,1,0:T(8,128)(2,1)} async-done(((bf16[64,16,1024]{2,1,0:T(8,128)(2,1)}), bf16[64,16,2048]{2,1,0:T(8,128)(2,1)}) %all-gather.3.cloned.1.call-update) | async-done | bytes 4194320 | tf_op jit(solution)/shard_map/all_gather | solution.py:55
  120.7 2.8 %gather_fusion = bf16[22,16,2048]{2,1,0:T(8,128)(2,1)S(1)} fusion(bf16[64,16,2048]{2,1,0:T(8,128)(2,1)} %all-gather.3.cloned.1.call-done, s32[1024]{0:T(1024)S(1)} %pad_clamp_fusion), kind=kCustom, calls=%fused_computation | custom fusion | bytes 2883672 | tf_op jit(solution)/shard_map/jit(_take)/gather | solution.py:56
  123.5 0.3 bitcast_select_fusion
  123.8 4.4 %fusion.10 = bf16[44,8,8,128]{3,1,2,0:T(8,128)(2,1)S(1)} fusion(bf16[352,2048]{1,0:T(8,128)(2,1)S(1)} %bitcast_select_fusion, bf16[2048,1024]{1,0:T(8,128)(2,1)} %param.9), kind=kOutput, calls=%fused_computation.25 | convolution fusion | flops 1476755456 | bytes 6356992 | tf_op jit(solution)/shard_map/dot_general | solution.py:58
  128.2 0.1 copy.111
  128.4 2.0 fusion.41
  130.4 2.4 %fusion.13 = bf16[11,32,8,128]{3,1,2,0:T(8,128)(2,1)S(1)} fusion(bf16[11,64,8,128]{3,2,1,0:T(8,128)(2,1)} %bitcast.106, f32[11,8,64,32]{2,3,1,0:T(8,128)} %get-tuple-element.7, f32[11,8,64]{2,1,0:T(8,128)S(1)} %get-tuple-element.6), kind=kOutput, calls=%fused_computation.28 | convolution fusion | flops 46858240 | bytes 2906112 | tf_op jit(solution)/shard_map/chtu,cthd->cuhd/dot_general | solution.py:92
  132.8 0.3 copy.107
  133.1 0.3 copy-done.7
  133.4 0.9 copy-done.4
  134.3 1.7 fusion.11
  136.0 0.0 copy-start.2
  136.0 0.1 copy.113
  136.2 1.2 copy-done.2
  137.4 1.3 fusion.1
  138.7 0.9 fusion.9
  139.6 0.5 fusion.12
  140.1 0.3 copy.105
  140.3 1.4 copy-done.6
  141.7 1.7 fusion.20
  143.4 3.3 %convolution_add_fusion = f32[352,2048]{1,0:T(8,128)} fusion(f32[352,2048]{1,0:T(8,128)S(1)} %fusion.20, bf16[2048,1024]{1,0:T(8,128)(2,1)S(1)} %copy-done.7, bf16[44,8,8,128]{3,2,1,0:T(8,128)(2,1)S(1)} %bitcast.111), kind=kOutput, calls=%fused_computation.8 | convolution fusion | flops 1477115904 | bytes 10682368 | tf_op jit(solution)/shard_map/dot_general | solution.py:100
  146.7 0.0 reduce-scatter.2.cloned.1.call-update
  146.8 17.5 %reduce-scatter.2.cloned.1.call-done = f32[22,16,1024]{2,1,0:T(8,128)} async-done(((f32[22,16,2048]{2,1,0:T(8,128)}), f32[22,16,1024]{2,1,0:T(8,128)}) %reduce-scatter.2.cloned.1.call-update) | async-done | bytes 1441808 | tf_op jit(solution)/shard_map/reduce_scatter | solution.py:103
  164.3 1.4 convert_element_type.63
  165.7 1.6 broadcast_in_dim.34
  167.4 4.6 %scatter_fusion = bf16[64,16,1024]{2,1,0:T(8,128)(2,1)} fusion(bf16[64,16,1024]{2,1,0:T(8,128)(2,1)} %broadcast_in_dim.34, s32[22]{0:T(128)S(1)} %fusion.38, bf16[22,16,1024]{2,1,0:T(8,128)(2,1)S(1)} %convert_element_type.63), kind=kCustom, calls=%fused_computation.1 | custom fusion | bytes 2162776 | tf_op jit(solution)/shard_map/scatter | solution.py:111
  171.9 9.9 %all-to-all-start.1 = ((bf16[32,2,16,1024]{3,2,1,0:T(8,128)(2,1)}), bf16[32,2,16,1024]{3,2,1,0:T(8,128)(2,1)S(1)}, u32[]{:S(2)}, u32[]{:S(2)}) async-start(bf16[32,2,16,1024]{3,2,1,0:T(8,128)(2,1)} %bitcast.13), calls=%async_computation.2 | async-start | bytes 4194304 | tf_op jit(solution)/shard_map/all_to_all | solution.py:114
  181.9 0.6 fusion.7
  182.5 1.1 copy.103
  183.6 1.5 copy.150
  185.1 47.2 %all-to-all-done.1 = bf16[32,2,16,1024]{3,2,1,0:T(8,128)(2,1)S(1)} async-done(((bf16[32,2,16,1024]{3,2,1,0:T(8,128)(2,1)}), bf16[32,2,16,1024]{3,2,1,0:T(8,128)(2,1)S(1)}, u32[]{:S(2)}, u32[]{:S(2)}) %all-to-all-start.1) | async-done | bytes 2097184 | tf_op jit(solution)/shard_map/all_to_all | solution.py:114
  232.3 1.2 copy.118
  233.5 0.5 convolution_convert_fusion.1
  234.1 0.3 copy.119
  234.4 0.8 slice.2
  (26 shorter events, 0.3 us)
Async XLA Ops:
  7.2 113.5 %all-gather.3.cloned.1.call-start = ((), (), s32[]{:S(2)}) async-start(), calls=%async_computation.3 | async-start | bytes 6291456 | tf_op jit(solution)/shard_map/all_gather | solution.py:55
  104.5 0.7 copy-start.5
  104.5 1.6 copy-start
  104.6 59.7 %reduce-scatter.2.cloned.1.call-start = ((), (), s32[]{:S(2)}) async-start(), calls=%async_computation.4 | async-start | bytes 4325376 | tf_op jit(solution)/shard_map/reduce_scatter | solution.py:103
  106.2 1.4 copy-start.1
  123.8 4.4 %copy-start.3 = (bf16[352,2048]{1,0:T(8,128)(2,1)}, bf16[352,2048]{1,0:T(8,128)(2,1)S(1)}, u32[]{:S(2)}) copy-start(bf16[352,2048]{1,0:T(8,128)(2,1)S(1)} %bitcast_select_fusion) | copy-start | bytes 4325380
  130.4 3.1 %copy-start.7 = (bf16[2048,1024]{1,0:T(8,128)(2,1)S(1)}, bf16[2048,1024]{1,0:T(8,128)(2,1)}, u32[]{:S(2)}) copy-start(bf16[2048,1024]{1,0:T(8,128)(2,1)} %param.10) | copy-start | bytes 12582916
  132.8 1.5 copy-start.4
  134.3 1.9 copy-start.8
  136.0 1.4 copy-start.2
  139.5 2.2 copy-start.6
  171.9 60.4 %all-to-all-start.1 = ((bf16[32,2,16,1024]{3,2,1,0:T(8,128)(2,1)}), bf16[32,2,16,1024]{3,2,1,0:T(8,128)(2,1)S(1)}, u32[]{:S(2)}, u32[]{:S(2)}) async-start(bf16[32,2,16,1024]{3,2,1,0:T(8,128)(2,1)} %bitcast.13), calls=%async_computation.2 | async-start | bytes 4194304 | tf_op jit(solution)/shard_map/all_to_all | solution.py:114
Sparse Core Ops, SparseCore 0:
  104.7 15.9 all-gather.2
  146.9 17.3 reduce-scatter.1
where the time goes:
time: 243 us; the launch traced here: 242 us
  blocking collectives  93.1 us (38%)
  waiting for transfers between devices  76.3 us (31%)
  local copies, waits for them, and re-layouts  25.6 us (11%)
  matrix products  20 us (8%)
  between operations  14.4 us (6%)
  starting transfers between devices  10.2 us (4%)
    all_to_all x1, waiting for transfers between devices, on_device(): lax.all_to_all(returning, 'seq', split_axis=0, concat_axis=0, tiled=True)  47.2 us
    all_to_all x1, blocking collectives, on_device(): lax.all_to_all(outgoing, 'seq', split_axis=0, concat_axis=0, tiled=True)  46.8 us
    all_gather x1, blocking collectives, on_device(): lax.all_gather(neighbours, 'seq', axis=0, tiled=True)  46.3 us
    reduce_scatter x1, waiting for transfers between devices, on_device(): lax.psum_scatter(partial_value.reshape(ref_count, neighbour_len, full_wid...  17.5 us
    unnamed x28, local copies, waits for them, and re-layouts  12.9 us
    all_gather x1, waiting for transfers between devices, on_device(): whole = lax.all_gather(flat_arrived, 'head', axis=2, tiled=True)  11.6 us
    all_to_all x1, starting transfers between devices, on_device(): lax.all_to_all(returning, 'seq', split_axis=0, concat_axis=0, tiled=True)  9.91 us
  transfers between devices with their start and end apart: 3, of which 3 were waited for; matrix products, arithmetic and copies ran while one was open for 3% of the time, Pallas kernels for 0%

commit v1 on v0

--- a/solution.py
+++ b/solution.py
@@ -6,6 +6,13 @@
 
 D = 2048
 HEADS = 16
+
+
+def gather_over(block, mesh_axis, along):
+    size = lax.axis_size(mesh_axis)
+    pieces = jnp.stack([block for _ in range(size)])
+    pieces = lax.all_to_all(pieces, mesh_axis, split_axis=0, concat_axis=0)
+    return jnp.concatenate(pieces, axis=along)
 
 
 def slot_ranks(owner_ids):
@@ -30,7 +37,7 @@
     scaling = 1.0 / math.sqrt(head_size)
     capacity = max(2, ref_count // seq_count)
     slot_count = seq_count * capacity
-    all_lists = lax.all_gather(neighbours, "seq", axis=0, tiled=True).reshape(seq_count, ref_count)
+    all_lists = gather_over(neighbours, "seq", 0).reshape(seq_count, ref_count)
     owner_table = all_lists // rows_here
     local_table = all_lists % rows_here
     rank_table = slot_ranks(owner_table)

time: 243 us -> 224 us (0.922)
  blocking collectives: 93.1 us -> 53.4 us
  starting transfers between devices: 10.2 us -> 21.7 us
  waiting for transfers between devices: 76.3 us -> 84.6 us
    all_gather x1 -> x0, blocking collectives: 46.3 us -> none  [on_device(): lax.all_gather(neighbours, 'seq', axis=0, tiled=True)]
    all_to_all x0 -> x1, starting transfers between devices: none -> 11.5 us  [gather_over(): pieces = lax.all_to_all(pieces, mesh_axis, split_axis=0, concat_axis=0)]
    all_to_all x0 -> x1, waiting for transfers between devices: none -> 8.46 us  [gather_over(): pieces = lax.all_to_all(pieces, mesh_axis, split_axis=0, concat_axis=0)]
    all_to_all x1, blocking collectives: 46.8 us -> 53.4 us  [on_device(): lax.all_to_all(outgoing, 'seq', split_axis=0, concat_axis=0, tiled=True)]
  transfers between devices with their start and end apart: 3 -> 4, of which waited for: 3 -> 4; matrix products, arithmetic and copies ran while one was open for 3% -> 3% of each run, Pallas kernels for 0% -> 0%
where the time goes in v1:
time: 224 us; the launch traced here: 223 us
  waiting for transfers between devices  84.6 us (38%)
  blocking collectives  53.4 us (24%)
  local copies, waits for them, and re-layouts  26.9 us (12%)
  starting transfers between devices  21.7 us (10%)
  matrix products  20 us (9%)
  between operations  14.4 us (6%)
  other arithmetic  2.26 us (1%)
    all_to_all x1, blocking collectives, on_device(): lax.all_to_all(outgoing, 'seq', split_axis=0, concat_axis=0, tiled=True)  53.4 us
    all_to_all x1, waiting for transfers between devices, on_device(): lax.all_to_all(returning, 'seq', split_axis=0, concat_axis=0, tiled=True)  47.2 us
    reduce_scatter x1, waiting for transfers between devices, on_device(): lax.psum_scatter(partial_value.reshape(ref_count, neighbour_len, full_wid...  17.5 us
    unnamed x28, local copies, waits for them, and re-layouts  12.9 us
    all_to_all x1, starting transfers between devices, gather_over(): pieces = lax.all_to_all(pieces, mesh_axis, split_axis=0, concat_axis=0)  11.5 us
    all_gather x1, waiting for transfers between devices, on_device(): whole = lax.all_gather(flat_arrived, 'head', axis=2, tiled=True)  11.3 us
    all_to_all x1, starting transfers between devices, on_device(): lax.all_to_all(returning, 'seq', split_axis=0, concat_axis=0, tiled=True)  9.91 us
    all_to_all x1, waiting for transfers between devices, gather_over(): pieces = lax.all_to_all(pieces, mesh_axis, split_axis=0, concat_axis=0)  8.46 us
  transfers between devices with their start and end apart: 4, of which 4 were waited for; matrix products, arithmetic and copies ran while one was open for 3% of the time, Pallas kernels for 0%

profile of v1, /device:TPU:2, one launch (start us, length us, event | category | flops | bytes accessed | tf_op | source)
XLA Modules:
  0.0 223.3 jit_solution(3722127002867488645)
XLA Ops:
  7.2 1.3 stack.2
  8.5 11.5 %all-to-all-start = ((s32[32,11,2]{1,2,0:T(2,128)}), s32[32,11,2]{1,2,0:T(2,128)S(1)}, u32[]{:S(2)}, u32[]{:S(2)}) async-start(s32[32,11,2]{1,2,0:T(2,128)} %stack.2), calls=%async_computation | async-start | bytes 65536 | tf_op jit(solution)/shard_map/all_to_all | solution.py:14
  20.0 0.0 all-gather.2.cloned.1.call-start
  20.0 1.0 pad.1
  21.1 0.3 copy.132
  21.3 8.5 %all-to-all-done = s32[32,11,2]{1,2,0:T(2,128)S(1)} async-done(((s32[32,11,2]{1,2,0:T(2,128)}), s32[32,11,2]{1,2,0:T(2,128)S(1)}, u32[]{:S(2)}, u32[]{:S(2)}) %all-to-all-start) | async-done | bytes 2848 | tf_op jit(solution)/shard_map/all_to_all | solution.py:14
  29.8 0.1 copy.111
  30.0 0.2 convert_reduce_fusion
  30.3 0.1 copy.116
  30.4 0.1 eq.78
  30.5 0.1 copy.115
  30.6 0.1 and.96
  30.7 0.7 convolution_convert_fusion
  31.5 1.2 copy.133
  32.7 53.4 %all_to_all.15 = bf16[32,2,16,1024]{3,2,1,0:T(8,128)(2,1)} all-to-all(bf16[32,2,16,1024]{3,2,1,0:T(8,128)(2,1)S(1)} %bitcast.93), channel_id=1, replica_groups=mesh['seq'=32,'head'=2,'dp'=4] {'seq'}, dimensions={0} | all-to-all | bytes 4194304 | tf_op jit(solution)/shard_map/all_to_all | solution.py:60
  86.1 0.0 all-gather.2.cloned.1.call-update
  86.1 0.2 reduce-scatter.2.cloned.1.call-start
  86.3 0.4 copy-done.5
  86.8 0.1 copy.110
  86.9 0.1 div.57
  86.9 0.1 div.60
  87.0 0.1 copy.109
  87.2 0.1 and.88
  87.2 0.1 and.100
  87.4 0.2 convert_reduce_fusion.1
  87.5 0.1 broadcast_in_dim.25
  87.6 0.1 broadcast_in_dim.26
  87.7 0.4 copy.135
  88.1 0.9 copy-done.1
  89.1 1.5 copy.137
  90.6 11.3 %all-gather.2.cloned.1.call-done = bf16[64,16,2048]{2,1,0:T(8,128)(2,1)} async-done(((bf16[64,16,1024]{2,1,0:T(8,128)(2,1)}), bf16[64,16,2048]{2,1,0:T(8,128)(2,1)}) %all-gather.2.cloned.1.call-update) | async-done | bytes 4194320 | tf_op jit(solution)/shard_map/all_gather | solution.py:62
  102.0 2.8 %gather_fusion = bf16[22,16,2048]{2,1,0:T(8,128)(2,1)S(1)} fusion(bf16[64,16,2048]{2,1,0:T(8,128)(2,1)} %all-gather.2.cloned.1.call-done, s32[1024]{0:T(1024)S(1)} %pad_clamp_fusion), kind=kCustom, calls=%fused_computation | custom fusion | bytes 2883672 | tf_op jit(solution)/shard_map/jit(_take)/gather | solution.py:63
  104.8 0.3 bitcast_select_fusion
  105.1 4.4 %fusion.10 = bf16[44,8,8,128]{3,1,2,0:T(8,128)(2,1)S(1)} fusion(bf16[352,2048]{1,0:T(8,128)(2,1)S(1)} %bitcast_select_fusion, bf16[2048,1024]{1,0:T(8,128)(2,1)} %param.9), kind=kOutput, calls=%fused_computation.25 | convolution fusion | flops 1476755456 | bytes 6356992 | tf_op jit(solution)/shard_map/dot_general | solution.py:65
  109.5 0.1 copy.134
  109.7 2.0 fusion.41
  111.7 2.4 %fusion.13 = bf16[11,32,8,128]{3,1,2,0:T(8,128)(2,1)S(1)} fusion(bf16[11,64,8,128]{3,2,1,0:T(8,128)(2,1)} %bitcast.105, f32[11,8,64,32]{2,3,1,0:T(8,128)} %get-tuple-element.7, f32[11,8,64]{2,1,0:T(8,128)S(1)} %get-tuple-element.6), kind=kOutput, calls=%fused_computation.28 | convolution fusion | flops 46858240 | bytes 2906112 | tf_op jit(solution)/shard_map/chtu,cthd->cuhd/dot_general | solution.py:99
  114.1 0.3 copy.130
  114.4 0.3 copy-done.7
  114.7 0.9 copy-done.4
  115.6 1.7 fusion.11
  117.3 0.1 copy.136
  117.5 1.2 copy-done.2
  118.7 1.3 fusion.1
  120.0 0.9 fusion.9
  120.8 0.5 fusion.12
  121.3 0.3 copy.128
  121.6 1.4 copy-done.6
  123.0 1.7 fusion.20
  124.7 3.3 %convolution_add_fusion = f32[352,2048]{1,0:T(8,128)} fusion(f32[352,2048]{1,0:T(8,128)S(1)} %fusion.20, bf16[2048,1024]{1,0:T(8,128)(2,1)S(1)} %copy-done.7, bf16[44,8,8,128]{3,2,1,0:T(8,128)(2,1)S(1)} %bitcast.110), kind=kOutput, calls=%fused_computation.8 | convolution fusion | flops 1477115904 | bytes 10682368 | tf_op jit(solution)/shard_map/dot_general | solution.py:107
  128.0 0.0 reduce-scatter.2.cloned.1.call-update
  128.1 17.5 %reduce-scatter.2.cloned.1.call-done = f32[22,16,1024]{2,1,0:T(8,128)} async-done(((f32[22,16,2048]{2,1,0:T(8,128)}), f32[22,16,1024]{2,1,0:T(8,128)}) %reduce-scatter.2.cloned.1.call-update) | async-done | bytes 1441808 | tf_op jit(solution)/shard_map/reduce_scatter | solution.py:110
  145.6 1.4 convert_element_type.63
  147.0 1.6 broadcast_in_dim.34
  148.6 4.6 %scatter_fusion = bf16[64,16,1024]{2,1,0:T(8,128)(2,1)} fusion(bf16[64,16,1024]{2,1,0:T(8,128)(2,1)} %broadcast_in_dim.34, s32[22]{0:T(128)S(1)} %fusion.38, bf16[22,16,1024]{2,1,0:T(8,128)(2,1)S(1)} %convert_element_type.63), kind=kCustom, calls=%fused_computation.1 | custom fusion | bytes 2162776 | tf_op jit(solution)/shard_map/scatter | solution.py:118
  153.2 9.9 %all-to-all-start.2 = ((bf16[32,2,16,1024]{3,2,1,0:T(8,128)(2,1)}), bf16[32,2,16,1024]{3,2,1,0:T(8,128)(2,1)S(1)}, u32[]{:S(2)}, u32[]{:S(2)}) async-start(bf16[32,2,16,1024]{3,2,1,0:T(8,128)(2,1)} %bitcast.12), calls=%async_computation.3 | async-start | bytes 4194304 | tf_op jit(solution)/shard_map/all_to_all | solution.py:121
  163.2 0.6 fusion.7
  163.8 1.1 copy.126
  164.9 1.5 copy.173
  166.4 47.2 %all-to-all-done.2 = bf16[32,2,16,1024]{3,2,1,0:T(8,128)(2,1)S(1)} async-done(((bf16[32,2,16,1024]{3,2,1,0:T(8,128)(2,1)}), bf16[32,2,16,1024]{3,2,1,0:T(8,128)(2,1)S(1)}, u32[]{:S(2)}, u32[]{:S(2)}) %all-to-all-start.2) | async-done | bytes 2097184 | tf_op jit(solution)/shard_map/all_to_all | solution.py:121
  213.6 1.2 copy.141
  214.8 0.5 convolution_convert_fusion.1
  215.4 0.3 copy.142
  215.7 0.8 slice.2
  (28 shorter events, 0.3 us)
Async XLA Ops:
  8.5 21.3 %all-to-all-start = ((s32[32,11,2]{1,2,0:T(2,128)}), s32[32,11,2]{1,2,0:T(2,128)S(1)}, u32[]{:S(2)}, u32[]{:S(2)}) async-start(s32[32,11,2]{1,2,0:T(2,128)} %stack.2), calls=%async_computation | async-start | bytes 65536 | tf_op jit(solution)/shard_map/all_to_all | solution.py:14
  20.0 82.0 %all-gather.2.cloned.1.call-start = ((), (), s32[]{:S(2)}) async-start(), calls=%async_computation.4 | async-start | bytes 6291456 | tf_op jit(solution)/shard_map/all_gather | solution.py:62
  86.1 0.7 copy-start.5
  86.1 1.6 copy-start
  86.1 59.5 %reduce-scatter.2.cloned.1.call-start = ((), (), s32[]{:S(2)}) async-start(), calls=%async_computation.5 | async-start | bytes 4325376 | tf_op jit(solution)/shard_map/reduce_scatter | solution.py:110
  87.7 1.4 copy-start.1
  105.1 4.4 %copy-start.3 = (bf16[352,2048]{1,0:T(8,128)(2,1)}, bf16[352,2048]{1,0:T(8,128)(2,1)S(1)}, u32[]{:S(2)}) copy-start(bf16[352,2048]{1,0:T(8,128)(2,1)S(1)} %bitcast_select_fusion) | copy-start | bytes 4325380
  111.7 3.1 %copy-start.7 = (bf16[2048,1024]{1,0:T(8,128)(2,1)S(1)}, bf16[2048,1024]{1,0:T(8,128)(2,1)}, u32[]{:S(2)}) copy-start(bf16[2048,1024]{1,0:T(8,128)(2,1)} %param.10) | copy-start | bytes 12582916
  114.1 1.5 copy-start.4
  115.6 1.9 copy-start.8
  117.3 1.4 copy-start.2
  120.8 2.2 copy-start.6
  153.2 60.4 %all-to-all-start.2 = ((bf16[32,2,16,1024]{3,2,1,0:T(8,128)(2,1)}), bf16[32,2,16,1024]{3,2,1,0:T(8,128)(2,1)S(1)}, u32[]{:S(2)}, u32[]{:S(2)}) async-start(bf16[32,2,16,1024]{3,2,1,0:T(8,128)(2,1)} %bitcast.12), calls=%async_computation.3 | async-start | bytes 4194304 | tf_op jit(solution)/shard_map/all_to_all | solution.py:121
Sparse Core Ops, SparseCore 0:
  86.2 15.6 all-gather.1
  128.2 17.3 reduce-scatter.1
